TPU v7x, 512 devices: a whole 4x8x8 slice. The times are simulated.
512 devices in a mesh: row: 8 (over x, core), col: 64 (over z, y).
Axes of the slice: x: 4, y: 8, z: 8, core: 2. Of those that a mesh axis runs over, the one named last changes fastest.
Arguments:
- src_latent: bfloat16 [32, 32768], P(None, 'row'), may hold values from -6 to 6
- tgt_latent: bfloat16 [32, 131072], P(None, 'col'), may hold values from -6 to 6
- g_start: float32 [131072], P('col'), may hold values from -1.5 to 1.5
- pairs: int32 [8, 64, 8, 2], P('row', 'col'), may hold values from 0 to 7, as said below
- counts: int32 [8, 64], P('row', 'col'), may hold values from 1 to 8, as said below
Outputs:
- f_new: float32 [32768], P('row')
- g_new: float32 [131072], P('col')
- bary: float32 [32, 32768], P(None, 'row')
Inputs may be any that keep to these rules, and one draw needn't show every extreme that they name: Within one device's 8 slots all pairs are distinct; entry 0 is below 8 and entry 1 below 4. Every source block and every target block appears among the live slots of some device. `counts`: some device has exactly 8 live slots in every draw.
All inputs are finite; a program needn't handle non-finite values.
Results may differ from a plain program's by a relative error of at most 0.0012.
Values sent between devices are 32-bit elements; how exact they have to be, the bound alone decides.
No kernel may reach another device: no remote copies, remote signals or barrier semaphores. Data moves between devices by JAX's collectives and lax.ppermute only.
A program may use at most 64 MiB of HBM per device.

v0:
```python
import jax
import jax.numpy as jnp
from jax import lax
from jax.sharding import PartitionSpec as P

BLOCK = 512
epsilon = 0.01
very_low = -1e30


def body(src_latent, tgt_latent, g_start, pairs, counts):
    src_len = src_latent.shape[1]
    tgt_len = tgt_latent.shape[1]
    width = src_latent.shape[0]
    rows_all = src_len * lax.axis_size("row")
    cols_all = tgt_len * lax.axis_size("col")
    sq_src = jnp.sum(jnp.square(src_latent.astype(jnp.float32)), axis=0)
    sq_tgt = jnp.sum(jnp.square(tgt_latent.astype(jnp.float32)), axis=0)
    slots = pairs[0, 0]
    count = counts[0, 0]

    def tile_score(p, row_pot, col_pot):
        s_off = slots[p, 0] * BLOCK
        t_off = slots[p, 1] * BLOCK
        xs = lax.dynamic_slice_in_dim(src_latent, s_off, BLOCK, 1)
        ys = lax.dynamic_slice_in_dim(tgt_latent, t_off, BLOCK, 1)
        cross = lax.dot_general(
            xs, ys, (((0,), (0,)), ((), ())), preferred_element_type=jnp.float32
        )
        sx = lax.dynamic_slice_in_dim(sq_src, s_off, BLOCK)
        sy = lax.dynamic_slice_in_dim(sq_tgt, t_off, BLOCK)
        cost = (sx[:, None] + sy[None, :] - 2.0 * cross) / width
        shifted = -cost
        if row_pot is not None:
            shifted = shifted + lax.dynamic_slice_in_dim(row_pot, s_off, BLOCK)[:, None]
        if col_pot is not None:
            shifted = shifted + lax.dynamic_slice_in_dim(col_pot, t_off, BLOCK)[None, :]
        return (shifted / epsilon, s_off, t_off, ys)

    def expand(vec, axis):
        return vec[:, None] if axis == 1 else vec[None, :]

    def local_peak(row_pot, col_pot, axis, length):

        def step(p, peak):
            score, s_off, t_off, _ = tile_score(p, row_pot, col_pot)
            off = s_off if axis == 1 else t_off
            old = lax.dynamic_slice_in_dim(peak, off, BLOCK)
            return lax.dynamic_update_slice_in_dim(
                peak, jnp.maximum(old, jnp.max(score, axis=axis)), off, 0
            )

        return lax.fori_loop(0, count, step, jnp.full((length,), very_low, jnp.float32))

    def local_total(row_pot, col_pot, axis, length, peak):

        def step(p, total):
            score, s_off, t_off, _ = tile_score(p, row_pot, col_pot)
            off = s_off if axis == 1 else t_off
            top = expand(lax.dynamic_slice_in_dim(peak, off, BLOCK), axis)
            old = lax.dynamic_slice_in_dim(total, off, BLOCK)
            return lax.dynamic_update_slice_in_dim(
                total, old + jnp.sum(jnp.exp(score - top), axis=axis), off, 0
            )

        return lax.fori_loop(0, count, step, jnp.zeros((length,), jnp.float32))

    peak_f = lax.pmax(local_peak(None, g_start, 1, src_len), "col")
    total_f = lax.psum(local_total(None, g_start, 1, src_len, peak_f), "col")
    f_new = -epsilon * jnp.log(1.0 * rows_all) - epsilon * (peak_f + jnp.log(total_f))
    peak_g = lax.pmax(local_peak(f_new, None, 0, tgt_len), "row")
    total_g = lax.psum(local_total(f_new, None, 0, tgt_len, peak_g), "row")
    g_new = -epsilon * jnp.log(1.0 * cols_all) - epsilon * (peak_g + jnp.log(total_g))
    peak_b = lax.pmax(local_peak(None, g_new, 1, src_len), "col")

    def accumulate(p, carry):
        numer, denom = carry
        score, s_off, t_off, ys = tile_score(p, None, g_new)
        top = lax.dynamic_slice_in_dim(peak_b, s_off, BLOCK)
        weight = jnp.exp(score - top[:, None]).astype(jnp.bfloat16)
        part = lax.dot_general(
            ys, weight, (((1,), (1,)), ((), ())), preferred_element_type=jnp.float32
        )
        old = lax.dynamic_slice_in_dim(numer, s_off, BLOCK, 1)
        numer = lax.dynamic_update_slice_in_dim(numer, old + part, s_off, 1)
        old_den = lax.dynamic_slice_in_dim(denom, s_off, BLOCK)
        denom = lax.dynamic_update_slice_in_dim(
            denom, old_den + jnp.sum(weight.astype(jnp.float32), axis=1), s_off, 0
        )
        return (numer, denom)

    init = (jnp.zeros((width, src_len), jnp.float32), jnp.zeros((src_len,), jnp.float32))
    numer, denom = lax.fori_loop(0, count, accumulate, init)
    numer, denom = lax.psum((numer, denom), "col")
    bary = numer / denom[None, :]
    return (f_new, g_new, bary)


def solution(mesh):
    in_specs = (
        P(None, "row"),
        P(None, "col"),
        P("col"),
        P("row", "col", None, None),
        P("row", "col"),
    )
    out_specs = (P("row"), P("col"), P(None, "row"))
    return jax.shard_map(body, mesh=mesh, in_specs=in_specs, out_specs=out_specs, check_vma=False)
```

profile of v0, /device:TPU:4, one launch (start us, length us, event | category | flops | bytes accessed | tf_op | source)
XLA Modules:
  0.0 1290.6 jit_solution(17436968615771430454)
XLA Ops:
  7.2 1.0 multiply_reduce_fusion.1
  8.2 1.1 multiply_reduce_fusion
  9.3 0.6 copy-done.1
  10.0 25.1 %while.62 = (s32[]{:T(128)}, f32[4096]{0:T(1024)S(1)}, s32[]{:T(128)}, s32[8,2]{0,1:T(2,128)S(1)}, f32[4096]{0:T(1024)S(1)}, /*index=5*/f32[2048]{0:T(1024)S(1)}...) while((s32[]{:T(128)}, f32[4096]{0:T(1024)S(1)}, ...), condition=%wide.region_4.0_spmd, body=%wide.region_2.0_spmd.sunk | while | flops 18874380 | bytes 92479 | solution.py:53
  10.7 0.7 constant_dynamic-slice_fusion.18
  14.2 0.7 constant_dynamic-slice_fusion.18
  17.6 0.7 constant_dynamic-slice_fusion.18
  21.1 0.7 constant_dynamic-slice_fusion.18
  24.6 0.7 constant_dynamic-slice_fusion.18
  28.1 0.7 constant_dynamic-slice_fusion.18
  31.6 0.7 constant_dynamic-slice_fusion.18
  35.1 274.0 %pmax.21 = f32[4096]{0:T(1024)S(1)} all-reduce(f32[4096]{0:T(1024)S(1)} %get-tuple-element.312), channel_id=1, replica_groups=mesh['row'=8,'col'=64] {'col'}, use_global_device_ids=true, to_apply=%region_5.0 | all-reduce | flops 4096 | bytes 32768 | tf_op jit(solution)/shard_map/pmax | solution.py:68
  309.0 26.3 %while.63 = (s32[]{:T(128)}, f32[4096]{0:T(1024)S(1)}, s32[]{:T(128)}, s32[8,2]{0,1:T(2,128)S(1)}, f32[4096]{0:T(1024)S(1)}, /*index=5*/f32[2048]{0:T(1024)S(1)}...) while((s32[]{:T(128)}, f32[4096]{0:T(1024)S(1)}, ...), condition=%wide.region_8.0_spmd, body=%wide.region_6.0_spmd.sunk | while | flops 19136524 | bytes 98635 | solution.py:66
  309.7 0.7 constant_dynamic-slice_fusion.19
  313.4 0.7 constant_dynamic-slice_fusion.19
  317.0 0.7 constant_dynamic-slice_fusion.19
  320.7 0.7 constant_dynamic-slice_fusion.19
  324.4 0.7 constant_dynamic-slice_fusion.19
  328.1 0.7 constant_dynamic-slice_fusion.19
  331.7 0.7 constant_dynamic-slice_fusion.19
  335.4 274.0 %psum.28 = f32[4096]{0:T(1024)S(1)} all-reduce(f32[4096]{0:T(1024)S(1)} %get-tuple-element.313), channel_id=1, replica_groups=mesh['row'=8,'col'=64] {'col'}, use_global_device_ids=true, to_apply=%region_9.0 | all-reduce | flops 4096 | bytes 32768 | tf_op jit(solution)/shard_map/psum | solution.py:69
  609.4 24.8 %while.64 = (s32[]{:T(128)}, f32[2048]{0:T(1024)S(1)}, s32[]{:T(128)}, s32[8,2]{0,1:T(2,128)S(1)}, f32[4096]{0:T(1024)S(1)}, /*index=5*/f32[2048]{0:T(1024)S(1)}...) while((s32[]{:T(128)}, f32[2048]{0:T(1024)S(1)}, ...), condition=%wide.region_12.0_spmd, body=%wide.region_10.0_spmd.sunk | while | flops 18874380 | bytes 92479 | solution.py:53
  610.0 0.6 constant_dynamic-slice_fusion.20
  634.1 10.3 pmax.22
  644.4 25.9 %while.65 = (s32[]{:T(128)}, f32[2048]{0:T(1024)S(1)}, s32[]{:T(128)}, s32[8,2]{0,1:T(2,128)S(1)}, f32[4096]{0:T(1024)S(1)}, /*index=5*/f32[2048]{0:T(1024)S(1)}...) while((s32[]{:T(128)}, f32[2048]{0:T(1024)S(1)}, ...), condition=%wide.region_16.0_spmd, body=%wide.region_14.0_spmd.sunk | while | flops 19136524 | bytes 98635 | solution.py:66
  670.4 10.3 psum.29
  680.7 24.8 %while.66 = (s32[]{:T(128)}, f32[4096]{0:T(1024)S(1)}, s32[]{:T(128)}, s32[8,2]{0,1:T(2,128)S(1)}, f32[4096]{0:T(1024)S(1)}, /*index=5*/f32[2048]{0:T(1024)S(1)}...) while((s32[]{:T(128)}, f32[4096]{0:T(1024)S(1)}, ...), condition=%wide.region_20.0_spmd, body=%wide.region_18.0_spmd.sunk | while | flops 18874380 | bytes 92479 | solution.py:53
  705.5 274.0 %pmax.23 = f32[4096]{0:T(1024)S(1)} all-reduce(f32[4096]{0:T(1024)S(1)} %get-tuple-element.316), channel_id=1, replica_groups=mesh['row'=8,'col'=64] {'col'}, use_global_device_ids=true, to_apply=%region_21.0 | all-reduce | flops 4096 | bytes 32768 | tf_op jit(solution)/shard_map/pmax | solution.py:74
  979.5 27.4 %while.67 = (s32[]{:T(128)}, f32[32,4096]{1,0:T(8,128)S(1)}, f32[4096]{0:T(1024)S(1)}, s32[]{:T(128)}, s32[8,2]{0,1:T(2,128)S(1)}, /*index=5*/bf16[32,2048]{1,0:...) while((s32[]{:T(128)}, f32[32,4096]{1,0:T(8,128)S(1)}, ...), condition=%wide.region_24.0_spmd, body=%wide.region_22.0_spmd.sunk | while | flops 36454412 | bytes 1311067 | solution.py:93
  1007.0 0.8 copy-done
  1007.8 274.1 %psum.31 = f32[4096]{0:T(1024)S(1)} all-reduce(f32[4096]{0:T(1024)S(1)} %get-tuple-element.318), channel_id=1, replica_groups=mesh['row'=8,'col'=64] {'col'}, use_global_device_ids=true, to_apply=%region_26.0 | all-reduce | flops 4096 | bytes 32768 | tf_op jit(solution)/shard_map/psum | solution.py:94
  1281.9 1.9 broadcast_divide_fusion
  (289 shorter events, 58.2 us)
Async XLA Ops:
  7.2 2.2 copy-start.3
  7.2 1274.7 %all-reduce.2.cloned.1.call-start = ((), (), s32[]{:S(2)}) async-start(), calls=%async_computation | async-start | bytes 1048576 | tf_op jit(solution)/shard_map/psum | solution.py:94
  8.2 1.1 copy-start.2
  9.3 0.7 copy-start.1
  9.3 0.7 copy-start.6
  670.4 10.3 copy-start.5
  1006.9 0.8 copy-start
  1007.0 0.8 copy-start.4
Sparse Core Ops, SparseCore 0:
  1007.9 148.3 all-reduce.1
where the time goes:
time: 1290 us
  blocking collectives  1120 us (87%)
  loops' own time  86.6 us (7%)
  local copies, waits for them, and re-layouts  38.4 us (3%)
  matrix products  22.9 us (2%)
  between operations  14.2 us (1%)
    psum x1, blocking collectives, body(): numer, denom = lax.psum((numer, denom), 'col')  274 us
    pmax x1, blocking collectives, body(): peak_f = lax.pmax(local_peak(None, g_start, 1, src_len), 'col')  274 us
    psum x1, blocking collectives, body(): total_f = lax.psum(local_total(None, g_start, 1, src_len, peak_f), 'col')  274 us
    pmax x1, blocking collectives, body(): peak_b = lax.pmax(local_peak(None, g_new, 1, src_len), 'col')  274 us
    another operation x3, loops' own time, local_peak(): lax.fori_loop(0, count, step, jnp.full((length,), very_low, jnp.float32))  43.2 us
    another operation x2, loops' own time, local_total(): return lax.fori_loop(0, count, step, jnp.zeros((length,), jnp.float32))  28.8 us
  transfers between devices with their start and end apart: 1, of which 0 were waited for; matrix products, arithmetic and copies ran while one was open for 0% of the time, Pallas kernels for 0%

commit v1 on v0

--- a/solution.py
+++ b/solution.py
@@ -66,7 +66,9 @@
         return lax.fori_loop(0, count, step, jnp.zeros((length,), jnp.float32))
 
     peak_f = lax.pmax(local_peak(None, g_start, 1, src_len), "col")
-    total_f = lax.psum(local_total(None, g_start, 1, src_len, peak_f), "col")
+    own = local_total(None, g_start, 1, src_len, peak_f)
+    parts = lax.all_gather(own, "col", axis=0, tiled=False)
+    total_f = parts.sum(axis=0)
     f_new = -epsilon * jnp.log(1.0 * rows_all) - epsilon * (peak_f + jnp.log(total_f))
     peak_g = lax.pmax(local_peak(f_new, None, 0, tgt_len), "row")
     total_g = lax.psum(local_total(f_new, None, 0, tgt_len, peak_g), "row")

time: 1290 us -> 1100 us (0.85)
  blocking collectives: 1120 us -> 843 us
  waiting for transfers between devices: 0.02 us -> 76.8 us
    psum x1 -> x0, blocking collectives: 274 us -> none  [body(): total_f = lax.psum(local_total(None, g_start, 1, src_len, peak_f), 'col')]
    all_gather x0 -> x1, waiting for transfers between devices: none -> 76.7 us  [body(): parts = lax.all_gather(own, 'col', axis=0, tiled=False)]
  transfers between devices with their start and end apart: 1 -> 2, of which waited for: 0 -> 1; matrix products, arithmetic and copies ran while one was open for 0% -> 0% of each run, Pallas kernels for 0% -> 0%
where the time goes in v1:
time: 1100 us
  blocking collectives  843 us (77%)
  loops' own time  87.9 us (8%)
  waiting for transfers between devices  76.8 us (7%)
  local copies, waits for them, and re-layouts  40.7 us (4%)
  matrix products  22.7 us (2%)
  between operations  14.3 us (1%)
  other arithmetic  11.1 us (1%)
    psum x1, blocking collectives, body(): numer, denom = lax.psum((numer, denom), 'col')  274 us
    pmax x1, blocking collectives, body(): peak_f = lax.pmax(local_peak(None, g_start, 1, src_len), 'col')  274 us
    pmax x1, blocking collectives, body(): peak_b = lax.pmax(local_peak(None, g_new, 1, src_len), 'col')  274 us
    all_gather x1, waiting for transfers between devices, body(): parts = lax.all_gather(own, 'col', axis=0, tiled=False)  76.7 us
    another operation x3, loops' own time, local_peak(): lax.fori_loop(0, count, step, jnp.full((length,), very_low, jnp.float32))  44.2 us
    another operation x2, loops' own time, local_total(): return lax.fori_loop(0, count, step, jnp.zeros((length,), jnp.float32))  29.1 us
  transfers between devices with their start and end apart: 2, of which 1 were waited for; matrix products, arithmetic and copies ran while one was open for 0% of the time, Pallas kernels for 0%

profile of v1, /device:TPU:4, one launch (start us, length us, event | category | flops | bytes accessed | tf_op | source)
XLA Modules:
  0.0 1096.1 jit_solution(12165422128243809526)
XLA Ops:
  7.2 1.1 multiply_reduce_fusion
  8.4 0.6 copy-done.1
  9.1 25.7 %while.62 = (s32[]{:T(128)}, f32[4096]{0:T(1024)S(1)}, s32[]{:T(128)}, s32[8,2]{0,1:T(2,128)S(1)}, f32[4096]{0:T(1024)S(1)}, /*index=5*/f32[2048]{0:T(1024)S(1)}...) while((s32[]{:T(128)}, f32[4096]{0:T(1024)S(1)}, ...), condition=%wide.region_4.0_spmd, body=%wide.region_2.0_spmd.sunk | while | flops 18874380 | bytes 92471 | solution.py:53
  9.8 0.7 constant_dynamic-slice_fusion.18
  13.4 0.7 constant_dynamic-slice_fusion.18
  16.9 0.7 constant_dynamic-slice_fusion.18
  20.5 0.7 constant_dynamic-slice_fusion.18
  24.1 0.7 constant_dynamic-slice_fusion.18
  27.7 0.7 constant_dynamic-slice_fusion.18
  31.3 0.7 constant_dynamic-slice_fusion.18
  34.8 274.0 %pmax.21 = f32[4096]{0:T(1024)S(1)} all-reduce(f32[4096]{0:T(1024)S(1)} %get-tuple-element.312), channel_id=1, replica_groups=mesh['row'=8,'col'=64] {'col'}, use_global_device_ids=true, to_apply=%region_5.0 | all-reduce | flops 4096 | bytes 32768 | tf_op jit(solution)/shard_map/pmax | solution.py:68
  308.8 26.1 %while.63 = (s32[]{:T(128)}, f32[4096]{0:T(1024)S(1)}, s32[]{:T(128)}, s32[8,2]{0,1:T(2,128)S(1)}, f32[4096]{0:T(1024)S(1)}, /*index=5*/f32[2048]{0:T(1024)S(1)}...) while((s32[]{:T(128)}, f32[4096]{0:T(1024)S(1)}, ...), condition=%wide.region_8.0_spmd, body=%wide.region_6.0_spmd.sunk | while | flops 19136524 | bytes 98627 | solution.py:66
  335.0 0.6 copy-done.4
  335.6 76.7 %all-gather.3.cloned.1.call-done = f32[262144]{0:T(1024)} async-done(((f32[4096]{0:T(1024)}), f32[262144]{0:T(1024)}) %all-gather.3.cloned.1.call-update) | async-done | bytes 1048592 | tf_op jit(solution)/shard_map/all_gather | solution.py:70
  412.4 1.4 reshape.52
  413.9 25.6 %while.64 = (s32[]{:T(128)}, f32[2048]{0:T(1024)S(1)}, s32[]{:T(128)}, s32[8,2]{0,1:T(2,128)S(1)}, f32[4096]{0:T(1024)S(1)}, /*index=5*/f32[2048]{0:T(1024)S(1)}...) while((s32[]{:T(128)}, f32[2048]{0:T(1024)S(1)}, ...), condition=%wide.region_12.0_spmd, body=%wide.region_10.0_spmd.sunk | while | flops 18874380 | bytes 92471 | solution.py:53
  414.6 0.7 constant_dynamic-slice_fusion.20
  418.2 0.7 constant_dynamic-slice_fusion.20
  421.7 0.7 constant_dynamic-slice_fusion.20
  425.3 0.7 constant_dynamic-slice_fusion.20
  428.8 0.7 constant_dynamic-slice_fusion.20
  432.4 0.7 constant_dynamic-slice_fusion.20
  436.0 0.7 constant_dynamic-slice_fusion.20
  439.5 10.3 pmax.22
  449.8 26.0 %while.65 = (s32[]{:T(128)}, f32[2048]{0:T(1024)S(1)}, s32[]{:T(128)}, s32[8,2]{0,1:T(2,128)S(1)}, f32[4096]{0:T(1024)S(1)}, /*index=5*/f32[2048]{0:T(1024)S(1)}...) while((s32[]{:T(128)}, f32[2048]{0:T(1024)S(1)}, ...), condition=%wide.region_16.0_spmd, body=%wide.region_14.0_spmd.sunk | while | flops 19136524 | bytes 98627 | solution.py:66
  475.8 10.3 psum.21
  486.1 24.9 %while.66 = (s32[]{:T(128)}, f32[4096]{0:T(1024)S(1)}, s32[]{:T(128)}, s32[8,2]{0,1:T(2,128)S(1)}, f32[4096]{0:T(1024)S(1)}, /*index=5*/f32[2048]{0:T(1024)S(1)}...) while((s32[]{:T(128)}, f32[4096]{0:T(1024)S(1)}, ...), condition=%wide.region_20.0_spmd, body=%wide.region_18.0_spmd.sunk | while | flops 18874380 | bytes 92471 | solution.py:53
  510.9 274.0 %pmax.23 = f32[4096]{0:T(1024)S(1)} all-reduce(f32[4096]{0:T(1024)S(1)} %get-tuple-element.316), channel_id=1, replica_groups=mesh['row'=8,'col'=64] {'col'}, use_global_device_ids=true, to_apply=%region_21.0 | all-reduce | flops 4096 | bytes 32768 | tf_op jit(solution)/shard_map/pmax | solution.py:76
  784.9 27.5 %while.67 = (s32[]{:T(128)}, f32[32,4096]{1,0:T(8,128)S(1)}, f32[4096]{0:T(1024)S(1)}, s32[]{:T(128)}, s32[8,2]{0,1:T(2,128)S(1)}, /*index=5*/bf16[32,2048]{1,0:...) while((s32[]{:T(128)}, f32[32,4096]{1,0:T(8,128)S(1)}, ...), condition=%wide.region_24.0_spmd, body=%wide.region_22.0_spmd.sunk | while | flops 36454412 | bytes 1311059 | solution.py:95
  812.5 0.8 copy-done
  813.3 274.1 %psum.23 = f32[4096]{0:T(1024)S(1)} all-reduce(f32[4096]{0:T(1024)S(1)} %get-tuple-element.318), channel_id=1, replica_groups=mesh['row'=8,'col'=64] {'col'}, use_global_device_ids=true, to_apply=%region_26.0 | all-reduce | flops 4096 | bytes 32768 | tf_op jit(solution)/shard_map/psum | solution.py:96
  1087.4 1.9 broadcast_divide_fusion
  (295 shorter events, 58.8 us)
Async XLA Ops:
  7.2 405.2 %all-gather.3.cloned.1.call-start = ((), (), s32[]{:S(2)}) async-start(), calls=%async_computation.1 | async-start | bytes 1064960 | tf_op jit(solution)/shard_map/all_gather | solution.py:70
  7.2 1.1 copy-start.2
  7.2 1.2 copy-start.3
  8.4 0.7 copy-start.1
  8.4 0.7 copy-start.7
  335.0 0.6 copy-start.4
  335.6 751.8 %all-reduce.2.cloned.1.call-start = ((), (), s32[]{:S(2)}) async-start(), calls=%async_computation | async-start | bytes 1048576 | tf_op jit(solution)/shard_map/psum | solution.py:96
  475.8 10.3 copy-start.6
  812.4 0.8 copy-start
  812.5 0.8 copy-start.5
Sparse Core Ops, SparseCore 0:
  335.7 76.6 all-gather.2
  813.4 148.3 all-reduce.1
